TPU v7x, 256 devices: a whole 4x4x8 slice. The times are simulated.
256 devices in a mesh: span: 8 (over z), ha: 8 (over x, core), wa: 4 (over y).
Axes of the slice: x: 4, y: 4, z: 8, core: 2. Of those that a mesh axis runs over, the one named last changes fastest.
Arguments:
- queries: bfloat16 [8, 3, 32, 48, 768], P('span', None, 'ha', 'wa'), may hold values from -5 to 5
- cache_keys: bfloat16 [8, 3, 32, 48, 768], P('span', None, 'ha', 'wa'), may hold values from -5 to 5
- cache_values: bfloat16 [8, 3, 32, 48, 768], P('span', None, 'ha', 'wa'), may hold values from -16 to 16
- grad_attended: bfloat16 [8, 3, 32, 48, 768], P('span', None, 'ha', 'wa'), may hold values from -16 to 16
- radius: int32 [6], replicated, may hold values from 1 to 2, as said below
- frame_count: int32 [8], replicated, may hold values from 1 to 3, as said below
Outputs:
- attended: bfloat16 [8, 3, 32, 48, 768], P('span', None, 'ha', 'wa')
- grad_queries: bfloat16 [8, 3, 32, 48, 768], P('span', None, 'ha', 'wa')
- grad_keys: bfloat16 [8, 3, 32, 48, 768], P('span', None, 'ha', 'wa')
- grad_values: bfloat16 [8, 3, 32, 48, 768], P('span', None, 'ha', 'wa')
Inputs may be any that keep to these rules, and one draw needn't show every extreme that they name: Some head has radius 2 and some other head has radius 1. Frame slots of block c at or past frame_count[c] hold padding; some block has all 3 slots live.
All inputs are finite; a program needn't handle non-finite values.
Results may differ from a plain program's by a relative error of at most 0.02.
Values may be sent and summed in bfloat16 or wider, within the bound.
A program may use at most 128 MiB of HBM per device.

v0:
```python
import math
import jax
import jax.numpy as jnp
from jax import lax
from jax.sharding import PartitionSpec as P

RMAX = 2


def padded(block, sides, width):
    for axis, dim in sides:
        count = lax.axis_size(axis)
        forward = [(i, i + 1) for i in range(count - 1)]
        backward = [(target, source) for source, target in forward]
        low = lax.ppermute(
            lax.slice_in_dim(block, block.shape[dim] - width, None, axis=dim), axis, forward
        )
        high = lax.ppermute(lax.slice_in_dim(block, 0, width, axis=dim), axis, backward)
        block = jnp.concatenate([low, block, high], axis=dim)
    return block


def near_table(radius, tile_h, tile_w, margin, first_row, first_col, full_h, full_w):
    rows_local = jnp.arange(tile_h)
    rows_wide = jnp.arange(tile_h + 2 * margin) - margin
    cols_local = jnp.arange(tile_w)
    cols_wide = jnp.arange(tile_w + 2 * margin) - margin
    gap_rows = jnp.abs(rows_local[:, None] - rows_wide[None, :])
    gap_cols = jnp.abs(cols_local[:, None] - cols_wide[None, :])
    inside_rows = (first_row + rows_wide >= 0) & (first_row + rows_wide < full_h)
    inside_cols = (first_col + cols_wide >= 0) & (first_col + cols_wide < full_w)
    reach = jnp.maximum(gap_rows[:, None, :, None], gap_cols[None, :, None, :])
    inside = inside_rows[:, None] & inside_cols[None, :]
    within = (reach[None] <= radius[:, None, None, None, None]) & inside[None, None, None]
    return within.reshape(
        radius.shape[0], tile_h * tile_w, (tile_h + 2 * margin) * (tile_w + 2 * margin)
    )


def with_frames(spatial, frame_live):
    heads, rows, columns = spatial.shape
    frames = frame_live.shape[0]
    joined = spatial[:, None, :, None, :] & frame_live[None, None, None, :, None]
    joined = jnp.broadcast_to(joined, (heads, frames, rows, frames, columns))
    return joined.reshape(heads, frames * rows, frames * columns)


def live_frames(frame_count, block_id, frames):
    picked = jnp.arange(frame_count.shape[0]) == block_id
    count = jnp.sum(jnp.where(picked, frame_count, 0))
    return jnp.arange(frames) < count


def over_tiles(advance, carried, piece):
    block_ids = jnp.arange(piece.shape[0], dtype=jnp.int32)

    def inner(current, item):
        return (advance(current, item[0], item[1]), None)

    result, _ = lax.scan(inner, carried, (piece, block_ids))
    return result


def shards(queries, cache_keys, cache_values, grad_attended, radius, frame_count):
    frames, tile_h, tile_w, width = queries.shape[1:]
    heads = radius.shape[0]
    depth = width // heads
    margin = RMAX
    scale = 1.0 / math.sqrt(depth)
    own_block = lax.axis_index("span")
    block_total = lax.axis_size("span")
    first_row = lax.axis_index("ha") * tile_h
    first_col = lax.axis_index("wa") * tile_w
    spatial = near_table(
        radius,
        tile_h,
        tile_w,
        margin,
        first_row,
        first_col,
        tile_h * lax.axis_size("ha"),
        tile_w * lax.axis_size("wa"),
    )
    local_rows = frames * tile_h * tile_w
    wide_rows = frames * (tile_h + 2 * margin) * (tile_w + 2 * margin)
    query_rows = queries.reshape(local_rows, heads, depth)
    key_local = cache_keys.reshape(local_rows, heads, depth)
    value_local = cache_values.reshape(local_rows, heads, depth)
    upstream = grad_attended.reshape(local_rows, heads, depth)
    key_mask = with_frames(
        jnp.transpose(spatial, (0, 2, 1)), live_frames(frame_count, own_block, frames)
    )
    bundle = jnp.concatenate([cache_keys, cache_values, queries, grad_attended], axis=4)

    def forward_step(carried, tile, block_id):

        def forward_run(current):
            top, total, accum = current
            key_rows = tile[..., :width].reshape(wide_rows, heads, depth)
            value_rows = tile[..., width : 2 * width].reshape(wide_rows, heads, depth)
            allowed = with_frames(spatial, live_frames(frame_count, block_id, frames))
            score = (
                jnp.einsum("qhd,khd->hqk", query_rows, key_rows, preferred_element_type=jnp.float32)
                * scale
            )
            score = jnp.where(allowed, score, -jnp.inf)
            new_top = jnp.maximum(top, jnp.max(score, axis=2))
            weight = jnp.exp(score - new_top[:, :, None])
            fading = jnp.exp(top - new_top)
            total = total * fading + jnp.sum(weight, axis=2)
            accum = accum * fading[:, :, None] + jnp.einsum(
                "hqk,khd->hqd",
                weight.astype(jnp.bfloat16),
                value_rows,
                preferred_element_type=jnp.float32,
            )
            return (new_top, total, accum)

        active = (block_id >= 0) & (block_id <= own_block)
        return lax.cond(active, forward_run, lambda current: current, carried)

    def query_grad_step(carried, tile, block_id):

        def query_run(current):
            key_rows = tile[..., :width].reshape(wide_rows, heads, depth)
            value_rows = tile[..., width : 2 * width].reshape(wide_rows, heads, depth)
            allowed = with_frames(spatial, live_frames(frame_count, block_id, frames))
            score = (
                jnp.einsum("qhd,khd->hqk", query_rows, key_rows, preferred_element_type=jnp.float32)
                * scale
            )
            prob = jnp.exp(jnp.where(allowed, score - log_total[:, :, None], -jnp.inf))
            push = jnp.einsum(
                "qhd,khd->hqk", upstream, value_rows, preferred_element_type=jnp.float32
            )
            slope = (prob * (push - delta[:, :, None])).astype(jnp.bfloat16)
            return current + jnp.einsum(
                "hqk,khd->hqd", slope, key_rows, preferred_element_type=jnp.float32
            )

        active = (block_id >= 0) & (block_id <= own_block)
        return lax.cond(active, query_run, lambda current: current, carried)

    def key_grad_step(carried, tile, block_id):

        def key_run(current):
            grad_k, grad_v = current
            asking = tile[..., -2 * width : -width].reshape(wide_rows, heads, depth)
            asking_grad = tile[..., -width:].reshape(wide_rows, heads, depth)
            stat_tile = lax.dynamic_index_in_dim(
                stats_all, jnp.clip(block_id, 0, block_total - 1), 0, keepdims=False
            )
            stat_rows = stat_tile.reshape(wide_rows, 2 * heads)
            row_lse = jnp.transpose(stat_rows[:, :heads])
            row_delta = jnp.transpose(stat_rows[:, heads:])
            score = (
                jnp.einsum("qhd,khd->hqk", asking, key_local, preferred_element_type=jnp.float32)
                * scale
            )
            prob = jnp.exp(jnp.where(key_mask, score - row_lse[:, :, None], -jnp.inf))
            grad_v = grad_v + jnp.einsum(
                "hqk,qhd->khd",
                prob.astype(jnp.bfloat16),
                asking_grad,
                preferred_element_type=jnp.float32,
            )
            push = jnp.einsum(
                "qhd,khd->hqk", asking_grad, value_local, preferred_element_type=jnp.float32
            )
            slope = (prob * (push - row_delta[:, :, None])).astype(jnp.bfloat16)
            grad_k = grad_k + jnp.einsum(
                "hqk,qhd->khd", slope, asking, preferred_element_type=jnp.float32
            )
            return (grad_k, grad_v)

        active = (block_id >= own_block) & (block_id < block_total)
        return lax.cond(active, key_run, lambda current: current, carried)

    start_state = (
        jnp.full((heads, local_rows), -jnp.inf, jnp.float32),
        jnp.zeros((heads, local_rows), jnp.float32),
        jnp.zeros((heads, local_rows, depth), jnp.float32),
    )
    everything = lax.all_gather(bundle, "span", axis=0, tiled=True)
    wide_all = padded(everything, (("ha", 2), ("wa", 3)), RMAX)
    top, total, accum = over_tiles(forward_step, start_state, wide_all)
    attended_rows = jnp.transpose((accum / total[:, :, None]).astype(jnp.bfloat16), (1, 0, 2))
    log_total = top + jnp.log(total)
    delta = jnp.einsum("qhd,qhd->hq", upstream, attended_rows, preferred_element_type=jnp.float32)
    stats = jnp.concatenate([jnp.transpose(log_total), jnp.transpose(delta)], axis=1)
    stats = stats.reshape(1, frames, tile_h, tile_w, 2 * heads)
    stat_wide = padded(stats, (("ha", 2), ("wa", 3)), RMAX)
    stats_all = lax.all_gather(stat_wide, "span", axis=0, tiled=True)
    query_start = jnp.zeros((heads, local_rows, depth), jnp.float32)
    key_start = (
        jnp.zeros((local_rows, heads, depth), jnp.float32),
        jnp.zeros((local_rows, heads, depth), jnp.float32),
    )
    grad_q = over_tiles(query_grad_step, query_start, wide_all)
    grad_k, grad_v = over_tiles(key_grad_step, key_start, wide_all)
    final = (1, frames, tile_h, tile_w, width)
    attended = attended_rows.reshape(final)
    grad_queries = jnp.transpose(grad_q * scale, (1, 0, 2)).astype(jnp.bfloat16).reshape(final)
    grad_keys = (grad_k * scale).astype(jnp.bfloat16).reshape(final)
    grad_values = grad_v.astype(jnp.bfloat16).reshape(final)
    return (attended, grad_queries, grad_keys, grad_values)


def solution(mesh):
    placed = (
        P("span", None, "ha", "wa", None),
        P("span", None, "ha", "wa", None),
        P("span", None, "ha", "wa", None),
        P("span", None, "ha", "wa", None),
        P(),
        P(),
    )
    return jax.shard_map(
        shards,
        mesh=mesh,
        in_specs=placed,
        out_specs=(
            P("span", None, "ha", "wa", None),
            P("span", None, "ha", "wa", None),
            P("span", None, "ha", "wa", None),
            P("span", None, "ha", "wa", None),
        ),
        check_vma=False,
    )
```

profile of v0, /device:TPU:2, one launch (start us, length us, event | category | flops | bytes accessed | tf_op | source)
XLA Modules:
  0.0 646.9 jit_solution(17913290227682815183)
XLA Ops:
  7.2 2.6 pad_maximum_fusion.4
  9.8 84.9 %all-gather.2.cloned.1.call-done = bf16[8,3,4,12,3072]{4,2,3,1,0:T(4,128)(2,1)} async-done(((bf16[1,3,4,12,3072]{4,2,3,1,0:T(4,128)(2,1)}), bf16[8,3,4,12,3072]{4,2,3,1,0:T(4,128)(2,1)}) %all-gather.2.cloned.1.call-update) | async-done | bytes 7077904 | tf_op jit(solution)/shard_map/all_gather | solution.py:184
  94.7 9.5 %fusion.57 = (bf16[8,3,2,12,3072]{4,2,3,1,0:T(2,128)(2,1)S(1)}, bf16[8,3,2,12,3072]{4,2,3,1,0:T(2,128)(2,1)S(1)}) fusion(bf16[8,3,4,12,3072]{4,2,3,1,0:T(4,128)(2,1)} %all-gather.2.cloned.1.call-done), kind=kLoop, calls=%fused_computation.100 | loop fusion | bytes 14155776 | tf_op jit(solution)/shard_map/slice | solution.py:16
  108.2 3.8 copy.86
  112.0 4.4 collective-permute-start.1
  116.3 32.7 %collective-permute-done = bf16[8,3,2,12,3072]{4,0,3,2,1:T(8,128)(2,1)S(1)} collective-permute-done((bf16[8,3,2,12,3072]{4,0,3,2,1:T(8,128)(2,1)S(1)}, bf16[8,3,2,12,3072]{4,0,3,2,1:T(8,128)(2,1)S(1)}, u32[]{:S(2)}, u32[]{:S(2)}) %collective-permute-start) | collective-permute-done | bytes 3538976 | tf_op jit(solution)/shard_map/ppermute | solution.py:15
  149.0 3.6 copy.87
  155.2 5.6 copy.88
  160.9 5.3 pad_maximum_fusion.3
  166.2 4.8 collective-permute-start.2
  198.0 22.7 %collective-permute-done.2 = bf16[8,3,8,2,3072]{4,2,3,1,0:T(8,128)(2,1)} collective-permute-done((bf16[8,3,8,2,3072]{4,2,3,1,0:T(8,128)(2,1)}, bf16[8,3,8,2,3072]{4,2,3,1,0:T(8,128)(2,1)}, u32[]{:S(2)}, u32[]{:S(2)}) %collective-permute-start.2) | collective-permute-done | bytes 2359328 | tf_op jit(solution)/shard_map/ppermute | solution.py:15
  220.7 6.0 collective-permute-done.3
  226.8 13.9 %pad_maximum_fusion = bf16[8,3,8,16,3072]{4,2,3,1,0:T(8,128)(2,1)S(1)} fusion(bf16[8,3,8,2,3072]{4,2,3,1,0:T(8,128)(2,1)} %collective-permute-done.3, bf16[8,3,2,12,3072]{4,2,3,1,0:T(2,128)(2,1)} %copy-done, bf16[8,3,4,12,3072]{4,2,3,1,0:T(4,128)(2,1)} %all-gather.2.cloned.1.call-done, bf16[8,3,2,12,3072]{4,2,3,1,0:T(2,128)(2,1)S(1)} %copy.87, ...), kind=kLoop, calls=%fused_computation.67 | loop fusion | flops 94371840 | bytes 37748736 | tf_op jit(solution)/shard_map/concatenate | solution.py:19
  240.7 12.6 %copy.90 = bf16[8,3,8,16,3072]{4,3,2,1,0:T(8,128)(2,1)} copy(bf16[8,3,8,16,3072]{4,2,3,1,0:T(8,128)(2,1)S(1)} %pad_maximum_fusion) | data formatting | bytes 37748736
  253.4 26.6 %while.42 = (s32[]{:T(128)}, f32[6,144]{1,0:T(8,128)S(1)}, f32[6,144]{1,0:T(8,128)S(1)}, f32[6,144,128]{2,1,0:T(8,128)S(1)}, s32[8]{0:T(128)S(1)}, /*index=5*/s3...) while((s32[]{:T(128)}, f32[6,144]{1,0:T(8,128)S(1)}, ...), condition=%wide.region_6.7_spmd.clone, body=%wide.region_0.6_spmd.clone.sunk | while | flops 172599008 | bytes 17480200 | solution.py:60
  255.3 11.1 %conditional.9 = ((f32[6,144]{1,0:T(8,128)S(1)}, f32[6,144]{1,0:T(8,128)S(1)}, f32[6,144,128]{2,1,0:T(8,128)S(1)})) conditional(s32[]{:T(128)} %convert_element_type.76, (f32[6,144]{1,0:T(8,128)S(1)}, f32[6,144]{1,0:T(8,128)S(1)}, f32[6,144,128]{2,1,0:T(8,128)S(1)}) %tuple.115, (s32[4,12,8,16]{3,2,1,0:T(8,128)S(1)}, s32[]{:T(128)}, s32[8]{0:T(128)}, ...), branch_computations={%region_1.1_spmd, %region_2.0_spmd} | conditional | flops 172599008 | bytes 17479918 | solution.py:120
  285.1 3.5 collective-permute-start.5
  290.0 29.6 %while.43 = (s32[]{:T(128)}, f32[6,144,128]{2,1,0:T(8,128)}, s32[8]{0:T(128)}, s32[]{:T(128)}, s32[8]{0:T(128)}, /*index=5*/bf16[8,3,8,16,3072]{4,3,2,1,0:T(8,12...) while((s32[]{:T(128)}, f32[6,144,128]{2,1,0:T(8,128)}, ...), condition=%wide.region_11.12_spmd.clone, body=%wide.region_7.11_spmd.clone.sunk | while | flops 257089568 | bytes 18095392 | solution.py:60
  292.3 11.0 %conditional.10 = (f32[6,144,128]{2,1,0:T(8,128)}) conditional(s32[]{:T(128)} %convert_element_type.77, f32[6,144,128]{2,1,0:T(8,128)} %get-tuple-element.945, (s32[4,12,8,16]{3,2,1,0:T(8,128)S(1)}, s32[]{:T(128)}, s32[8]{0:T(128)}, bf16[8,3,8,16,3072]{4,3,2,1,0:T(8,128)(2,1)}, s32[]{:T(128)}, /*index=5*/bf16[144,6,128]{2,0,1:T(8,128)(2,1)}, ...), branch_computations={%region_8.8_spmd, %region_9.10_spmd} | conditional | flops 257089568 | bytes 18095118 | solution.py:142
  300.6 2.7 fusion.23
  327.4 2.8 collective-permute-done.7
  331.2 180.3 %all_gather.7 = f32[8,3,8,16,12]{3,2,4,1,0:T(8,128)S(1)} all-gather(f32[1,3,8,16,12]{3,2,4,1,0:T(8,128)S(1)} %copy.99), channel_id=1, replica_groups=mesh['span'=8,'ha'=8,'wa'=4] {'span'}, dimensions={0}, use_global_device_ids=true | all-gather | bytes 165888 | tf_op jit(solution)/shard_map/all_gather | solution.py:193
  513.5 122.9 %while.44 = (s32[]{:T(128)}, f32[144,6,128]{2,0,1:T(8,128)S(1)}, f32[144,6,128]{2,0,1:T(8,128)}, s32[8]{0:T(128)S(1)}, s32[]{:T(128)}, /*index=5*/bf16[8,3,8,16,...) while((s32[]{:T(128)}, f32[144,6,128]{2,0,1:T(8,128)S(1)}, ...), condition=%wide.region_16.17_spmd.clone, body=%wide.region_13.16_spmd.clone.sunk | while | flops 342282240 | bytes 23095652 | solution.py:60
  515.4 13.5 %conditional.11 = ((f32[144,6,128]{2,0,1:T(8,128)S(1)}, f32[144,6,128]{2,0,1:T(8,128)})) conditional(s32[]{:T(128)} %convert_element_type.78, (f32[144,6,128]{2,0,1:T(8,128)S(1)}, f32[144,6,128]{2,0,1:T(8,128)}) %tuple.120, (bf16[8,3,8,16,3072]{4,3,2,1,0:T(8,128)(2,1)}, s32[]{:T(128)}, bf16[144,6,128]{2,0,1:T(8,128)(2,1)}, s32[]{:T(128)}, ...), branch_computations={%region_14.14_spmd, %region_15.15_spmd} | conditional | flops 342282240 | bytes 23095408 | solution.py:177
  530.8 13.5 %conditional.11 = ((f32[144,6,128]{2,0,1:T(8,128)S(1)}, f32[144,6,128]{2,0,1:T(8,128)})) conditional(s32[]{:T(128)} %convert_element_type.78, (f32[144,6,128]{2,0,1:T(8,128)S(1)}, f32[144,6,128]{2,0,1:T(8,128)}) %tuple.120, (bf16[8,3,8,16,3072]{4,3,2,1,0:T(8,128)(2,1)}, s32[]{:T(128)}, bf16[144,6,128]{2,0,1:T(8,128)(2,1)}, s32[]{:T(128)}, ...), branch_computations={%region_14.14_spmd, %region_15.15_spmd} | conditional | flops 342282240 | bytes 23095408 | solution.py:177
  539.4 2.6 fusion.40
  546.1 13.5 %conditional.11 = ((f32[144,6,128]{2,0,1:T(8,128)S(1)}, f32[144,6,128]{2,0,1:T(8,128)})) conditional(s32[]{:T(128)} %convert_element_type.78, (f32[144,6,128]{2,0,1:T(8,128)S(1)}, f32[144,6,128]{2,0,1:T(8,128)}) %tuple.120, (bf16[8,3,8,16,3072]{4,3,2,1,0:T(8,128)(2,1)}, s32[]{:T(128)}, bf16[144,6,128]{2,0,1:T(8,128)(2,1)}, s32[]{:T(128)}, ...), branch_computations={%region_14.14_spmd, %region_15.15_spmd} | conditional | flops 342282240 | bytes 23095408 | solution.py:177
  561.5 13.5 %conditional.11 = ((f32[144,6,128]{2,0,1:T(8,128)S(1)}, f32[144,6,128]{2,0,1:T(8,128)})) conditional(s32[]{:T(128)} %convert_element_type.78, (f32[144,6,128]{2,0,1:T(8,128)S(1)}, f32[144,6,128]{2,0,1:T(8,128)}) %tuple.120, (bf16[8,3,8,16,3072]{4,3,2,1,0:T(8,128)(2,1)}, s32[]{:T(128)}, bf16[144,6,128]{2,0,1:T(8,128)(2,1)}, s32[]{:T(128)}, ...), branch_computations={%region_14.14_spmd, %region_15.15_spmd} | conditional | flops 342282240 | bytes 23095408 | solution.py:177
  576.9 13.5 %conditional.11 = ((f32[144,6,128]{2,0,1:T(8,128)S(1)}, f32[144,6,128]{2,0,1:T(8,128)})) conditional(s32[]{:T(128)} %convert_element_type.78, (f32[144,6,128]{2,0,1:T(8,128)S(1)}, f32[144,6,128]{2,0,1:T(8,128)}) %tuple.120, (bf16[8,3,8,16,3072]{4,3,2,1,0:T(8,128)(2,1)}, s32[]{:T(128)}, bf16[144,6,128]{2,0,1:T(8,128)(2,1)}, s32[]{:T(128)}, ...), branch_computations={%region_14.14_spmd, %region_15.15_spmd} | conditional | flops 342282240 | bytes 23095408 | solution.py:177
  592.2 13.5 %conditional.11 = ((f32[144,6,128]{2,0,1:T(8,128)S(1)}, f32[144,6,128]{2,0,1:T(8,128)})) conditional(s32[]{:T(128)} %convert_element_type.78, (f32[144,6,128]{2,0,1:T(8,128)S(1)}, f32[144,6,128]{2,0,1:T(8,128)}) %tuple.120, (bf16[8,3,8,16,3072]{4,3,2,1,0:T(8,128)(2,1)}, s32[]{:T(128)}, bf16[144,6,128]{2,0,1:T(8,128)(2,1)}, s32[]{:T(128)}, ...), branch_computations={%region_14.14_spmd, %region_15.15_spmd} | conditional | flops 342282240 | bytes 23095408 | solution.py:177
  607.6 13.5 %conditional.11 = ((f32[144,6,128]{2,0,1:T(8,128)S(1)}, f32[144,6,128]{2,0,1:T(8,128)})) conditional(s32[]{:T(128)} %convert_element_type.78, (f32[144,6,128]{2,0,1:T(8,128)S(1)}, f32[144,6,128]{2,0,1:T(8,128)}) %tuple.120, (bf16[8,3,8,16,3072]{4,3,2,1,0:T(8,128)(2,1)}, s32[]{:T(128)}, bf16[144,6,128]{2,0,1:T(8,128)(2,1)}, s32[]{:T(128)}, ...), branch_computations={%region_14.14_spmd, %region_15.15_spmd} | conditional | flops 342282240 | bytes 23095408 | solution.py:177
  622.9 13.5 %conditional.11 = ((f32[144,6,128]{2,0,1:T(8,128)S(1)}, f32[144,6,128]{2,0,1:T(8,128)})) conditional(s32[]{:T(128)} %convert_element_type.78, (f32[144,6,128]{2,0,1:T(8,128)S(1)}, f32[144,6,128]{2,0,1:T(8,128)}) %tuple.120, (bf16[8,3,8,16,3072]{4,3,2,1,0:T(8,128)(2,1)}, s32[]{:T(128)}, bf16[144,6,128]{2,0,1:T(8,128)(2,1)}, s32[]{:T(128)}, ...), branch_computations={%region_14.14_spmd, %region_15.15_spmd} | conditional | flops 342282240 | bytes 23095408 | solution.py:177
  (299 shorter events, 191.3 us)
Async XLA Ops:
  7.2 87.6 %all-gather.2.cloned.1.call-start = ((), (), s32[]{:S(2)}) async-start(), calls=%async_computation | async-start | bytes 7962624 | tf_op jit(solution)/shard_map/all_gather | solution.py:184
  106.2 42.8 %collective-permute-start = (bf16[8,3,2,12,3072]{4,0,3,2,1:T(8,128)(2,1)S(1)}, bf16[8,3,2,12,3072]{4,0,3,2,1:T(8,128)(2,1)S(1)}, u32[]{:S(2)}, u32[]{:S(2)}) collective-permute-start(bf16[8,3,2,12,3072]{4,0,3,2,1:T(8,128)(2,1)S(1)} %copy.85), channel_id=1, source_target_pairs={{0,4},{4,8},{8,12},{12,16},{16,20},{20,24},{24,28},{1,5},{5,9},{9,... | collective-permute-start | bytes 10616840 | tf_op jit(solution)/shard_map/ppermute | solution.py:15
  108.1 52.7 %slice-start = ((s8[7077888]{0:T(1024)(128)(4,1)}), s8[4194304]{0:T(1024)(128)(4,1)S(1)}, s32[]{:S(2)}) async-start(s8[7077888]{0:T(1024)(128)(4,1)} %bitcast.91), calls=%async_computation.1 | async-start | bytes 8388608
  112.0 48.9 %slice-start.1 = ((s8[7077888]{0:T(1024)(128)(4,1)}), s8[2883584]{0:T(1024)(128)(4,1)S(1)}, s32[]{:S(2)}) async-start(s8[7077888]{0:T(1024)(128)(4,1)} %bitcast.91), calls=%async_computation.2 | async-start | bytes 5767168
  112.0 43.2 %collective-permute-start.1 = (bf16[8,3,2,12,3072]{4,0,3,2,1:T(8,128)(2,1)}, bf16[8,3,2,12,3072]{4,0,3,2,1:T(8,128)(2,1)}, u32[]{:S(2)}, u32[]{:S(2)}) collective-permute-start(bf16[8,3,2,12,3072]{4,0,3,2,1:T(8,128)(2,1)} %copy.86), channel_id=1, source_target_pairs={{4,0},{8,4},{12,8},{16,12},{20,16},{24,20},{28,24},{5,1},{9,5},{13... | collective-permute-start | bytes 10616840 | tf_op jit(solution)/shard_map/ppermute | solution.py:18
  160.8 5.3 copy-start
  160.8 11.6 %copy-start.5 = (bf16[1,3,4,12,768]{4,2,3,1,0:T(4,128)(2,1)S(1)}, bf16[1,3,4,12,768]{4,2,3,1,0:T(4,128)(2,1)}, u32[]{:S(2)}) copy-start(bf16[1,3,4,12,768]{4,2,3,1,0:T(4,128)(2,1)} %param.18) | copy-start | bytes 663556
  160.9 12.3 %copy-start.6 = (bf16[1,3,4,12,768]{4,2,3,1,0:T(4,128)(2,1)S(1)}, bf16[1,3,4,12,768]{4,2,3,1,0:T(4,128)(2,1)}, u32[]{:S(2)}) copy-start(bf16[1,3,4,12,768]{4,2,3,1,0:T(4,128)(2,1)} %param.21) | copy-start | bytes 663556
  160.9 13.0 %copy-start.7 = (bf16[1,3,4,12,768]{4,2,3,1,0:T(4,128)(2,1)S(1)}, bf16[1,3,4,12,768]{4,2,3,1,0:T(4,128)(2,1)}, u32[]{:S(2)}) copy-start(bf16[1,3,4,12,768]{4,2,3,1,0:T(4,128)(2,1)} %param.19) | copy-start | bytes 663556
  160.9 13.8 %copy-start.8 = (bf16[1,3,4,12,768]{4,2,3,1,0:T(4,128)(2,1)S(1)}, bf16[1,3,4,12,768]{4,2,3,1,0:T(4,128)(2,1)}, u32[]{:S(2)}) copy-start(bf16[1,3,4,12,768]{4,2,3,1,0:T(4,128)(2,1)} %param.20) | copy-start | bytes 663556
  166.2 54.5 %collective-permute-start.2 = (bf16[8,3,8,2,3072]{4,2,3,1,0:T(8,128)(2,1)}, bf16[8,3,8,2,3072]{4,2,3,1,0:T(8,128)(2,1)}, u32[]{:S(2)}, u32[]{:S(2)}) collective-permute-start(bf16[8,3,8,2,3072]{4,2,3,1,0:T(8,128)(2,1)} %get-tuple-element.644), channel_id=1, source_target_pairs={{0,1},{1,2},{2,3},{4,5},{5,6},{6,7},{8,9},{9,10},{10,11},{12,13},{... | collective-permute-start | bytes 7077896 | tf_op jit(solution)/shard_map/ppermute | solution.py:15
  170.9 55.8 %collective-permute-start.3 = (bf16[8,3,8,2,3072]{4,2,3,1,0:T(8,128)(2,1)}, bf16[8,3,8,2,3072]{4,2,3,1,0:T(8,128)(2,1)}, u32[]{:S(2)}, u32[]{:S(2)}) collective-permute-start(bf16[8,3,8,2,3072]{4,2,3,1,0:T(8,128)(2,1)} %get-tuple-element.645), channel_id=1, source_target_pairs={{1,0},{2,1},{3,2},{5,4},{6,5},{7,6},{9,8},{10,9},{11,10},{13,12},{... | collective-permute-start | bytes 7077896 | tf_op jit(solution)/shard_map/ppermute | solution.py:18
  175.4 21.0 %copy-start.11 = (s32[6]{0:T(128)S(1)}, s32[6]{0:T(128)}, u32[]{:S(2)}) copy-start(s32[6]{0:T(128)} %param.22) | copy-start | bytes 76
  183.2 10.6 %copy-start.12 = (pred[128]{0:T(512)(128)(4,1)S(1)}, pred[128]{0:T(512)(128)(4,1)}, u32[]{:S(2)}) copy-start(pred[128]{0:T(512)(128)(4,1)} %and.135) | copy-start | bytes 388
  240.7 12.7 %copy-start.1 = (s32[4,12,8,16]{3,2,1,0:T(8,128)S(1)}, s32[4,12,8,16]{3,2,1,0:T(8,128)}, u32[]{:S(2)}) copy-start(s32[4,12,8,16]{3,2,1,0:T(8,128)} %broadcast_maximum_fusion) | copy-start | bytes 73732
  282.9 36.7 %collective-permute-start.4 = (f32[1,3,2,12,12]{3,2,1,4,0:T(2,128)}, f32[1,3,2,12,12]{3,2,1,4,0:T(2,128)}, u32[]{:S(2)}, u32[]{:S(2)}) collective-permute-start(f32[1,3,2,12,12]{3,2,1,4,0:T(2,128)} %get-tuple-element.652), channel_id=1, source_target_pairs={{0,4},{4,8},{8,12},{12,16},{16,20},{20,24},{24,28},{1,5},{5,9},{9,... | collective-permute-start | bytes 10376 | tf_op jit(solution)/shard_map/ppermute | solution.py:15
  285.1 34.5 %collective-permute-start.5 = (f32[1,3,2,12,12]{3,2,1,4,0:T(2,128)}, f32[1,3,2,12,12]{3,2,1,4,0:T(2,128)}, u32[]{:S(2)}, u32[]{:S(2)}) collective-permute-start(f32[1,3,2,12,12]{3,2,1,4,0:T(2,128)} %get-tuple-element.653), channel_id=1, source_target_pairs={{4,0},{8,4},{12,8},{16,12},{20,16},{24,20},{28,24},{5,1},{9,5},{13... | collective-permute-start | bytes 10376 | tf_op jit(solution)/shard_map/ppermute | solution.py:18
  295.5 5.1 copy-start.10
  319.6 6.6 %copy-start.9 = (bf16[144,6,128]{2,0,1:T(8,128)(2,1)S(1)}, bf16[144,6,128]{2,0,1:T(8,128)(2,1)}, u32[]{:S(2)}) copy-start(bf16[144,6,128]{2,0,1:T(8,128)(2,1)} %get-tuple-element.649) | copy-start | bytes 663556
  320.7 6.7 %collective-permute-start.6 = (f32[1,3,8,2,12]{3,2,1,4,0:T(8,128)S(1)}, f32[1,3,8,2,12]{3,2,1,4,0:T(8,128)S(1)}, u32[]{:S(2)}, u32[]{:S(2)}) collective-permute-start(f32[1,3,8,2,12]{3,2,1,4,0:T(8,128)S(1)} %get-tuple-element.650), channel_id=1, source_target_pairs={{0,1},{1,2},{2,3},{4,5},{5,6},{6,7},{8,9},{9,10},{10,11},{12,13},{... | collective-permute-start | bytes 6920 | tf_op jit(solution)/shard_map/ppermute | solution.py:15
  322.7 7.5 %collective-permute-start.7 = (f32[1,3,8,2,12]{3,2,1,4,0:T(8,128)S(1)}, f32[1,3,8,2,12]{3,2,1,4,0:T(8,128)S(1)}, u32[]{:S(2)}, u32[]{:S(2)}) collective-permute-start(f32[1,3,8,2,12]{3,2,1,4,0:T(8,128)S(1)} %get-tuple-element.651), channel_id=1, source_target_pairs={{1,0},{2,1},{3,2},{5,4},{6,5},{7,6},{9,8},{10,9},{11,10},{13,12},{... | collective-permute-start | bytes 6920 | tf_op jit(solution)/shard_map/ppermute | solution.py:18
  526.6 2.2 copy-start.3
  530.8 2.0 copy-start.2
  542.0 2.2 copy-start.3
  557.4 2.2 copy-start.3
  561.5 2.0 copy-start.2
  572.7 2.2 copy-start.3
  588.1 2.2 copy-start.3
  592.2 2.0 copy-start.2
  603.5 2.2 copy-start.3
  618.8 2.2 copy-start.3
  634.2 2.2 copy-start.3
  (6 other events, 11.1 us)
Sparse Core Ops, SparseCore 0:
  10.0 84.7 all-gather.1
where the time goes:
time: 655 us; the launch traced here: 647 us
  blocking collectives  180 us (27%)
  waiting for transfers between devices  152 us (23%)
  local copies, waits for them, and re-layouts  147 us (22%)
  matrix products  55.1 us (8%)
  other arithmetic  39.6 us (6%)
  loops' own time  36.7 us (6%)
  starting transfers between devices  21.6 us (3%)
  between operations  14.7 us (2%)
    all_gather x1, blocking collectives, shards(): stats_all = lax.all_gather(stat_wide, 'span', axis=0, tiled=True)  180 us
    all_gather x1, waiting for transfers between devices, shards(): everything = lax.all_gather(bundle, 'span', axis=0, tiled=True)  84.9 us
    ppermute x4, waiting for transfers between devices, padded(): lax.ppermute(lax.slice_in_dim(block, block.shape[dim] - width, None, axis...  55.4 us
    another operation x3, loops' own time, over_tiles(): result, _ = lax.scan(inner, carried, (piece, block_ids))  30.3 us
    unnamed x36, local copies, waits for them, and re-layouts  26.6 us
    dot_general x8, matrix products, key_run(): jnp.einsum('hqk,qhd->khd', slope, asking, preferred_element_type=jnp.floa...  20.5 us
    squeeze x10, local copies, waits for them, and re-layouts, over_tiles(): result, _ = lax.scan(inner, carried, (piece, block_ids))  19.7 us
    dynamic_slice x24, local copies, waits for them, and re-layouts, over_tiles(): result, _ = lax.scan(inner, carried, (piece, block_ids))  18.6 us
  transfers between devices with their start and end apart: 9, of which 6 were waited for; matrix products, arithmetic and copies ran while one was open for 9% of the time, Pallas kernels for 0%

commit v1 on v0

--- a/solution.py
+++ b/solution.py
@@ -190,7 +190,9 @@
     stats = jnp.concatenate([jnp.transpose(log_total), jnp.transpose(delta)], axis=1)
     stats = stats.reshape(1, frames, tile_h, tile_w, 2 * heads)
     stat_wide = padded(stats, (("ha", 2), ("wa", 3)), RMAX)
-    stats_all = lax.all_gather(stat_wide, "span", axis=0, tiled=True)
+    stats_all = jnp.concatenate(
+        lax.all_to_all(jnp.stack([stat_wide] * lax.axis_size("span")), "span", 0, 0), axis=0
+    )
     query_start = jnp.zeros((heads, local_rows, depth), jnp.float32)
     key_start = (
         jnp.zeros((local_rows, heads, depth), jnp.float32),

time: 655 us -> 558 us (0.85)
  blocking collectives: 180 us -> 0 us
  starting transfers between devices: 21.6 us -> 99.4 us
  waiting for transfers between devices: 152 us -> 168 us
  local copies, waits for them, and re-layouts: 147 us -> 135 us
    all_gather x1 -> x0, blocking collectives: 180 us -> none  [shards(): stats_all = lax.all_gather(stat_wide, 'span', axis=0, tiled=True)]
    all_to_all x0 -> x1, starting transfers between devices: none -> 77.7 us  [shards(): lax.all_to_all(jnp.stack([stat_wide] * lax.axis_size('span')), 'span', 0, 0)]
    ppermute x4, waiting for transfers between devices: 55.4 us -> 69.2 us  [padded(): lax.ppermute(lax.slice_in_dim(block, block.shape[dim] - width, None, axis...]
    unnamed x36 -> x42, local copies, waits for them, and re-layouts: 26.6 us -> 22.2 us
  transfers between devices with their start and end apart: 9 -> 10, of which waited for: 6 -> 8; matrix products, arithmetic and copies ran while one was open for 9% -> 8% of each run, Pallas kernels for 0% -> 0%
where the time goes in v1:
time: 558 us; the launch traced here: 550 us
  waiting for transfers between devices  168 us (30%)
  local copies, waits for them, and re-layouts  135 us (24%)
  starting transfers between devices  99.4 us (18%)
  matrix products  55.2 us (10%)
  other arithmetic  38.9 us (7%)
  loops' own time  38 us (7%)
  between operations  14.7 us (3%)
    all_gather x1, waiting for transfers between devices, shards(): everything = lax.all_gather(bundle, 'span', axis=0, tiled=True)  84.9 us
    all_to_all x1, starting transfers between devices, shards(): lax.all_to_all(jnp.stack([stat_wide] * lax.axis_size('span')), 'span', 0, 0)  77.7 us
    ppermute x4, waiting for transfers between devices, padded(): lax.ppermute(lax.slice_in_dim(block, block.shape[dim] - width, None, axis...  69.2 us
    another operation x3, loops' own time, over_tiles(): result, _ = lax.scan(inner, carried, (piece, block_ids))  31.6 us
    unnamed x42, local copies, waits for them, and re-layouts  22.2 us
    dot_general x8, matrix products, key_run(): jnp.einsum('hqk,qhd->khd', slope, asking, preferred_element_type=jnp.floa...  20.6 us
    squeeze x10, local copies, waits for them, and re-layouts, over_tiles(): result, _ = lax.scan(inner, carried, (piece, block_ids))  19.7 us
    dot_general x8, matrix products, key_run(): jnp.einsum('hqk,qhd->khd', prob.astype(jnp.bfloat16), asking_grad, prefer...  17.8 us
  transfers between devices with their start and end apart: 10, of which 8 were waited for; matrix products, arithmetic and copies ran while one was open for 8% of the time, Pallas kernels for 0%

profile of v1, /device:TPU:2, one launch (start us, length us, event | category | flops | bytes accessed | tf_op | source)
XLA Modules:
  0.0 549.8 jit_solution(8473128701877446615)
XLA Ops:
  7.2 2.6 pad_maximum_fusion.4
  9.9 84.9 %all-gather.2.cloned.1.call-done = bf16[8,3,4,12,3072]{4,2,3,1,0:T(4,128)(2,1)} async-done(((bf16[1,3,4,12,3072]{4,2,3,1,0:T(4,128)(2,1)}), bf16[8,3,4,12,3072]{4,2,3,1,0:T(4,128)(2,1)}) %all-gather.2.cloned.1.call-update) | async-done | bytes 7077904 | tf_op jit(solution)/shard_map/all_gather | solution.py:184
  94.7 9.5 %fusion.57 = (bf16[8,3,2,12,3072]{4,2,3,1,0:T(2,128)(2,1)S(1)}, bf16[8,3,2,12,3072]{4,2,3,1,0:T(2,128)(2,1)S(1)}) fusion(bf16[8,3,4,12,3072]{4,2,3,1,0:T(4,128)(2,1)} %all-gather.2.cloned.1.call-done), kind=kLoop, calls=%fused_computation.100 | loop fusion | bytes 14155776 | tf_op jit(solution)/shard_map/slice | solution.py:16
  108.1 3.8 copy.52
  112.0 4.4 collective-permute-start.1
  116.3 32.7 %collective-permute-done = bf16[8,3,2,12,3072]{4,0,3,2,1:T(8,128)(2,1)S(1)} collective-permute-done((bf16[8,3,2,12,3072]{4,0,3,2,1:T(8,128)(2,1)S(1)}, bf16[8,3,2,12,3072]{4,0,3,2,1:T(8,128)(2,1)S(1)}, u32[]{:S(2)}, u32[]{:S(2)}) %collective-permute-start) | collective-permute-done | bytes 3538976 | tf_op jit(solution)/shard_map/ppermute | solution.py:15
  149.0 3.6 copy.53
  155.2 5.6 %copy.54 = bf16[8,3,2,12,3072]{4,2,3,1,0:T(2,128)(2,1)S(1)} copy(bf16[8,3,2,12,3072]{4,0,3,2,1:T(8,128)(2,1)} %collective-permute-done.1) | data formatting | bytes 7077888 | tf_op jit(solution)/shard_map/ppermute | solution.py:18
  160.9 5.3 pad_maximum_fusion.3
  166.1 4.9 collective-permute-start.2
  185.6 35.2 %collective-permute-done.2 = bf16[8,3,8,2,3072]{4,2,3,1,0:T(8,128)(2,1)} collective-permute-done((bf16[8,3,8,2,3072]{4,2,3,1,0:T(8,128)(2,1)}, bf16[8,3,8,2,3072]{4,2,3,1,0:T(8,128)(2,1)}, u32[]{:S(2)}, u32[]{:S(2)}) %collective-permute-start.2) | collective-permute-done | bytes 2359328 | tf_op jit(solution)/shard_map/ppermute | solution.py:15
  220.8 6.0 %collective-permute-done.3 = bf16[8,3,8,2,3072]{4,2,3,1,0:T(8,128)(2,1)} collective-permute-done((bf16[8,3,8,2,3072]{4,2,3,1,0:T(8,128)(2,1)}, bf16[8,3,8,2,3072]{4,2,3,1,0:T(8,128)(2,1)}, u32[]{:S(2)}, u32[]{:S(2)}) %collective-permute-start.3) | collective-permute-done | bytes 2359328 | tf_op jit(solution)/shard_map/ppermute | solution.py:18
  226.9 13.9 %pad_maximum_fusion = bf16[8,3,8,16,3072]{4,2,3,1,0:T(8,128)(2,1)S(1)} fusion(bf16[8,3,8,2,3072]{4,2,3,1,0:T(8,128)(2,1)} %collective-permute-done.3, bf16[8,3,2,12,3072]{4,2,3,1,0:T(2,128)(2,1)} %copy-done, bf16[8,3,4,12,3072]{4,2,3,1,0:T(4,128)(2,1)} %all-gather.2.cloned.1.call-done, bf16[8,3,2,12,3072]{4,2,3,1,0:T(2,128)(2,1)S(1)} %copy.53, ...), kind=kLoop, calls=%fused_computation.67 | loop fusion | flops 94371840 | bytes 37748736 | tf_op jit(solution)/shard_map/concatenate | solution.py:19
  240.8 12.6 %copy.56 = bf16[8,3,8,16,3072]{4,3,2,1,0:T(8,128)(2,1)} copy(bf16[8,3,8,16,3072]{4,2,3,1,0:T(8,128)(2,1)S(1)} %pad_maximum_fusion) | data formatting | bytes 37748736
  253.5 26.1 %while.42 = (s32[]{:T(128)}, f32[6,144]{1,0:T(8,128)S(1)}, f32[6,144]{1,0:T(8,128)S(1)}, f32[6,144,128]{2,1,0:T(8,128)S(1)}, s32[8]{0:T(128)S(1)}, /*index=5*/s3...) while((s32[]{:T(128)}, f32[6,144]{1,0:T(8,128)S(1)}, ...), condition=%wide.region_6.7_spmd.clone, body=%wide.region_0.6_spmd.clone.sunk | while | flops 172599008 | bytes 17480200 | solution.py:60
  255.4 10.7 %conditional.9 = ((f32[6,144]{1,0:T(8,128)S(1)}, f32[6,144]{1,0:T(8,128)S(1)}, f32[6,144,128]{2,1,0:T(8,128)S(1)})) conditional(s32[]{:T(128)} %convert_element_type.76, (f32[6,144]{1,0:T(8,128)S(1)}, f32[6,144]{1,0:T(8,128)S(1)}, f32[6,144,128]{2,1,0:T(8,128)S(1)}) %tuple.111, (s32[4,12,8,16]{3,2,1,0:T(8,128)S(1)}, s32[]{:T(128)}, s32[8]{0:T(128)S(1)}, ...), branch_computations={%region_1.1_spmd, %region_2.0_spmd} | conditional | flops 172599008 | bytes 17479918 | solution.py:120
  284.4 3.3 collective-permute-start.5
  294.9 4.7 collective-permute-done.7
  301.0 77.7 %all-to-all-start = ((f32[8,1,4608]{2,1,0:T(1,128)}), f32[8,1,4608]{2,1,0:T(1,128)}, u32[]{:S(2)}, u32[]{:S(2)}) async-start(f32[8,1,4608]{2,1,0:T(1,128)} %reshape.246), calls=%async_computation | async-start | bytes 294912 | tf_op jit(solution)/shard_map/all_to_all | solution.py:194
  382.4 25.7 %while.43 = (s32[]{:T(128)}, f32[6,144,128]{2,1,0:T(8,128)}, s32[8]{0:T(128)S(1)}, s32[]{:T(128)}, s32[8]{0:T(128)S(1)}, /*index=5*/bf16[8,3,8,16,3072]{4,3,2,1,...) while((s32[]{:T(128)}, f32[6,144,128]{2,1,0:T(8,128)}, ...), condition=%wide.region_11.12_spmd.clone, body=%wide.region_7.11_spmd.clone.sunk | while | flops 257089568 | bytes 16325865 | solution.py:60
  384.2 10.4 %conditional.10 = (f32[6,144,128]{2,1,0:T(8,128)}) conditional(s32[]{:T(128)} %convert_element_type.77, f32[6,144,128]{2,1,0:T(8,128)} %get-tuple-element.906, (s32[4,12,8,16]{3,2,1,0:T(8,128)S(1)}, s32[]{:T(128)}, s32[8]{0:T(128)S(1)}, bf16[8,3,8,16,3072]{4,3,2,1,0:T(8,128)(2,1)}, s32[]{:T(128)}, /*index=5*/bf16[144,6,128]{2,0,1:T(8,128)(2,1)}, ...), branch_computations={%region_8.8_spmd, %region_9.10_spmd} | conditional | flops 257089568 | bytes 16325590 | solution.py:142
  391.9 2.8 fusion.23
  416.3 122.9 %while.44 = (s32[]{:T(128)}, f32[144,6,128]{2,0,1:T(8,128)S(1)}, f32[144,6,128]{2,0,1:T(8,128)}, s32[8]{0:T(128)S(1)}, s32[]{:T(128)}, /*index=5*/bf16[8,3,8,16,...) while((s32[]{:T(128)}, f32[144,6,128]{2,0,1:T(8,128)S(1)}, ...), condition=%wide.region_16.17_spmd.clone, body=%wide.region_13.16_spmd.clone.sunk | while | flops 342282240 | bytes 23095652 | solution.py:60
  418.2 13.5 %conditional.11 = ((f32[144,6,128]{2,0,1:T(8,128)S(1)}, f32[144,6,128]{2,0,1:T(8,128)})) conditional(s32[]{:T(128)} %convert_element_type.78, (f32[144,6,128]{2,0,1:T(8,128)S(1)}, f32[144,6,128]{2,0,1:T(8,128)}) %tuple.116, (bf16[8,3,8,16,3072]{4,3,2,1,0:T(8,128)(2,1)}, s32[]{:T(128)}, bf16[144,6,128]{2,0,1:T(8,128)(2,1)}, s32[]{:T(128)}, ...), branch_computations={%region_14.14_spmd, %region_15.15_spmd} | conditional | flops 342282240 | bytes 23095408 | solution.py:177
  433.6 13.5 %conditional.11 = ((f32[144,6,128]{2,0,1:T(8,128)S(1)}, f32[144,6,128]{2,0,1:T(8,128)})) conditional(s32[]{:T(128)} %convert_element_type.78, (f32[144,6,128]{2,0,1:T(8,128)S(1)}, f32[144,6,128]{2,0,1:T(8,128)}) %tuple.116, (bf16[8,3,8,16,3072]{4,3,2,1,0:T(8,128)(2,1)}, s32[]{:T(128)}, bf16[144,6,128]{2,0,1:T(8,128)(2,1)}, s32[]{:T(128)}, ...), branch_computations={%region_14.14_spmd, %region_15.15_spmd} | conditional | flops 342282240 | bytes 23095408 | solution.py:177
  448.9 13.5 %conditional.11 = ((f32[144,6,128]{2,0,1:T(8,128)S(1)}, f32[144,6,128]{2,0,1:T(8,128)})) conditional(s32[]{:T(128)} %convert_element_type.78, (f32[144,6,128]{2,0,1:T(8,128)S(1)}, f32[144,6,128]{2,0,1:T(8,128)}) %tuple.116, (bf16[8,3,8,16,3072]{4,3,2,1,0:T(8,128)(2,1)}, s32[]{:T(128)}, bf16[144,6,128]{2,0,1:T(8,128)(2,1)}, s32[]{:T(128)}, ...), branch_computations={%region_14.14_spmd, %region_15.15_spmd} | conditional | flops 342282240 | bytes 23095408 | solution.py:177
  457.6 2.6 fusion.40
  464.3 13.5 %conditional.11 = ((f32[144,6,128]{2,0,1:T(8,128)S(1)}, f32[144,6,128]{2,0,1:T(8,128)})) conditional(s32[]{:T(128)} %convert_element_type.78, (f32[144,6,128]{2,0,1:T(8,128)S(1)}, f32[144,6,128]{2,0,1:T(8,128)}) %tuple.116, (bf16[8,3,8,16,3072]{4,3,2,1,0:T(8,128)(2,1)}, s32[]{:T(128)}, bf16[144,6,128]{2,0,1:T(8,128)(2,1)}, s32[]{:T(128)}, ...), branch_computations={%region_14.14_spmd, %region_15.15_spmd} | conditional | flops 342282240 | bytes 23095408 | solution.py:177
  479.7 13.5 %conditional.11 = ((f32[144,6,128]{2,0,1:T(8,128)S(1)}, f32[144,6,128]{2,0,1:T(8,128)})) conditional(s32[]{:T(128)} %convert_element_type.78, (f32[144,6,128]{2,0,1:T(8,128)S(1)}, f32[144,6,128]{2,0,1:T(8,128)}) %tuple.116, (bf16[8,3,8,16,3072]{4,3,2,1,0:T(8,128)(2,1)}, s32[]{:T(128)}, bf16[144,6,128]{2,0,1:T(8,128)(2,1)}, s32[]{:T(128)}, ...), branch_computations={%region_14.14_spmd, %region_15.15_spmd} | conditional | flops 342282240 | bytes 23095408 | solution.py:177
  495.1 13.5 %conditional.11 = ((f32[144,6,128]{2,0,1:T(8,128)S(1)}, f32[144,6,128]{2,0,1:T(8,128)})) conditional(s32[]{:T(128)} %convert_element_type.78, (f32[144,6,128]{2,0,1:T(8,128)S(1)}, f32[144,6,128]{2,0,1:T(8,128)}) %tuple.116, (bf16[8,3,8,16,3072]{4,3,2,1,0:T(8,128)(2,1)}, s32[]{:T(128)}, bf16[144,6,128]{2,0,1:T(8,128)(2,1)}, s32[]{:T(128)}, ...), branch_computations={%region_14.14_spmd, %region_15.15_spmd} | conditional | flops 342282240 | bytes 23095408 | solution.py:177
  510.4 13.5 %conditional.11 = ((f32[144,6,128]{2,0,1:T(8,128)S(1)}, f32[144,6,128]{2,0,1:T(8,128)})) conditional(s32[]{:T(128)} %convert_element_type.78, (f32[144,6,128]{2,0,1:T(8,128)S(1)}, f32[144,6,128]{2,0,1:T(8,128)}) %tuple.116, (bf16[8,3,8,16,3072]{4,3,2,1,0:T(8,128)(2,1)}, s32[]{:T(128)}, bf16[144,6,128]{2,0,1:T(8,128)(2,1)}, s32[]{:T(128)}, ...), branch_computations={%region_14.14_spmd, %region_15.15_spmd} | conditional | flops 342282240 | bytes 23095408 | solution.py:177
  525.8 13.5 %conditional.11 = ((f32[144,6,128]{2,0,1:T(8,128)S(1)}, f32[144,6,128]{2,0,1:T(8,128)})) conditional(s32[]{:T(128)} %convert_element_type.78, (f32[144,6,128]{2,0,1:T(8,128)S(1)}, f32[144,6,128]{2,0,1:T(8,128)}) %tuple.116, (bf16[8,3,8,16,3072]{4,3,2,1,0:T(8,128)(2,1)}, s32[]{:T(128)}, bf16[144,6,128]{2,0,1:T(8,128)(2,1)}, s32[]{:T(128)}, ...), branch_computations={%region_14.14_spmd, %region_15.15_spmd} | conditional | flops 342282240 | bytes 23095408 | solution.py:177
  (304 shorter events, 181.0 us)
Async XLA Ops:
  7.2 87.6 %all-gather.2.cloned.1.call-start = ((), (), s32[]{:S(2)}) async-start(), calls=%async_computation.1 | async-start | bytes 7962624 | tf_op jit(solution)/shard_map/all_gather | solution.py:184
  106.2 42.8 %collective-permute-start = (bf16[8,3,2,12,3072]{4,0,3,2,1:T(8,128)(2,1)S(1)}, bf16[8,3,2,12,3072]{4,0,3,2,1:T(8,128)(2,1)S(1)}, u32[]{:S(2)}, u32[]{:S(2)}) collective-permute-start(bf16[8,3,2,12,3072]{4,0,3,2,1:T(8,128)(2,1)S(1)} %copy.51), channel_id=1, source_target_pairs={{0,4},{4,8},{8,12},{12,16},{16,20},{20,24},{24,28},{1,5},{5,9},{9,... | collective-permute-start | bytes 10616840 | tf_op jit(solution)/shard_map/ppermute | solution.py:15
  108.1 52.7 %slice-start = ((s8[7077888]{0:T(1024)(128)(4,1)}), s8[4194304]{0:T(1024)(128)(4,1)S(1)}, s32[]{:S(2)}) async-start(s8[7077888]{0:T(1024)(128)(4,1)} %bitcast.99), calls=%async_computation.2 | async-start | bytes 8388608
  112.0 48.9 %slice-start.1 = ((s8[7077888]{0:T(1024)(128)(4,1)}), s8[2883584]{0:T(1024)(128)(4,1)S(1)}, s32[]{:S(2)}) async-start(s8[7077888]{0:T(1024)(128)(4,1)} %bitcast.99), calls=%async_computation.3 | async-start | bytes 5767168
  112.0 43.2 %collective-permute-start.1 = (bf16[8,3,2,12,3072]{4,0,3,2,1:T(8,128)(2,1)}, bf16[8,3,2,12,3072]{4,0,3,2,1:T(8,128)(2,1)}, u32[]{:S(2)}, u32[]{:S(2)}) collective-permute-start(bf16[8,3,2,12,3072]{4,0,3,2,1:T(8,128)(2,1)} %copy.52), channel_id=1, source_target_pairs={{4,0},{8,4},{12,8},{16,12},{20,16},{24,20},{28,24},{5,1},{9,5},{13... | collective-permute-start | bytes 10616840 | tf_op jit(solution)/shard_map/ppermute | solution.py:18
  160.8 5.3 copy-start
  160.8 11.7 %copy-start.5 = (bf16[1,3,4,12,768]{4,2,3,1,0:T(4,128)(2,1)S(1)}, bf16[1,3,4,12,768]{4,2,3,1,0:T(4,128)(2,1)}, u32[]{:S(2)}) copy-start(bf16[1,3,4,12,768]{4,2,3,1,0:T(4,128)(2,1)} %param.18) | copy-start | bytes 663556
  160.8 12.4 %copy-start.6 = (bf16[1,3,4,12,768]{4,2,3,1,0:T(4,128)(2,1)S(1)}, bf16[1,3,4,12,768]{4,2,3,1,0:T(4,128)(2,1)}, u32[]{:S(2)}) copy-start(bf16[1,3,4,12,768]{4,2,3,1,0:T(4,128)(2,1)} %param.21) | copy-start | bytes 663556
  166.1 18.0 %copy-start.11 = (s32[6]{0:T(128)S(1)}, s32[6]{0:T(128)}, u32[]{:S(2)}) copy-start(s32[6]{0:T(128)} %param.22) | copy-start | bytes 76
  166.1 54.7 %collective-permute-start.2 = (bf16[8,3,8,2,3072]{4,2,3,1,0:T(8,128)(2,1)}, bf16[8,3,8,2,3072]{4,2,3,1,0:T(8,128)(2,1)}, u32[]{:S(2)}, u32[]{:S(2)}) collective-permute-start(bf16[8,3,8,2,3072]{4,2,3,1,0:T(8,128)(2,1)} %get-tuple-element.605), channel_id=1, source_target_pairs={{0,1},{1,2},{2,3},{4,5},{5,6},{6,7},{8,9},{9,10},{10,11},{12,13},{... | collective-permute-start | bytes 7077896 | tf_op jit(solution)/shard_map/ppermute | solution.py:15
  171.0 55.8 %collective-permute-start.3 = (bf16[8,3,8,2,3072]{4,2,3,1,0:T(8,128)(2,1)}, bf16[8,3,8,2,3072]{4,2,3,1,0:T(8,128)(2,1)}, u32[]{:S(2)}, u32[]{:S(2)}) collective-permute-start(bf16[8,3,8,2,3072]{4,2,3,1,0:T(8,128)(2,1)} %get-tuple-element.606), channel_id=1, source_target_pairs={{1,0},{2,1},{3,2},{5,4},{6,5},{7,6},{9,8},{10,9},{11,10},{13,12},{... | collective-permute-start | bytes 7077896 | tf_op jit(solution)/shard_map/ppermute | solution.py:18
  240.8 12.7 %copy-start.1 = (s32[4,12,8,16]{3,2,1,0:T(8,128)S(1)}, s32[4,12,8,16]{3,2,1,0:T(8,128)}, u32[]{:S(2)}) copy-start(s32[4,12,8,16]{3,2,1,0:T(8,128)} %broadcast_maximum_fusion) | copy-start | bytes 73732
  240.8 12.7 %copy-start.12 = (s32[8]{0:T(128)S(1)}, s32[8]{0:T(128)}, u32[]{:S(2)}) copy-start(s32[8]{0:T(128)} %param.23) | copy-start | bytes 100
  281.8 96.8 %copy-start.10 = (pred[6,128,48]{1,2,0:T(8,128)(4,1)S(1)}, pred[6,128,48]{1,2,0:T(8,128)(4,1)}, u32[]{:S(2)}) copy-start(pred[6,128,48]{1,2,0:T(8,128)(4,1)} %compare_and_fusion.2) | copy-start | bytes 110596
  282.0 97.5 %copy-start.7 = (bf16[1,3,4,12,768]{4,2,3,1,0:T(4,128)(2,1)S(1)}, bf16[1,3,4,12,768]{4,2,3,1,0:T(4,128)(2,1)}, u32[]{:S(2)}) copy-start(bf16[1,3,4,12,768]{4,2,3,1,0:T(4,128)(2,1)} %param.19) | copy-start | bytes 663556
  282.0 6.3 %collective-permute-start.4 = (f32[1,3,2,12,12]{3,2,1,4,0:T(2,128)S(1)}, f32[1,3,2,12,12]{3,2,1,4,0:T(2,128)S(1)}, u32[]{:S(2)}, u32[]{:S(2)}) collective-permute-start(f32[1,3,2,12,12]{3,2,1,4,0:T(2,128)S(1)} %get-tuple-element.613), channel_id=1, source_target_pairs={{0,4},{4,8},{8,12},{12,16},{16,20},{20,24},{24,28},{1,5},{5,9},{9,... | collective-permute-start | bytes 10376 | tf_op jit(solution)/shard_map/ppermute | solution.py:15
  284.4 5.0 collective-permute-start.5
  289.4 90.1 %copy-start.8 = (bf16[1,3,4,12,768]{4,2,3,1,0:T(4,128)(2,1)S(1)}, bf16[1,3,4,12,768]{4,2,3,1,0:T(4,128)(2,1)}, u32[]{:S(2)}) copy-start(bf16[1,3,4,12,768]{4,2,3,1,0:T(4,128)(2,1)} %param.20) | copy-start | bytes 663556
  289.5 5.3 collective-permute-start.6
  291.6 8.0 %collective-permute-start.7 = (f32[1,3,8,2,12]{3,2,1,4,0:T(8,128)S(1)}, f32[1,3,8,2,12]{3,2,1,4,0:T(8,128)S(1)}, u32[]{:S(2)}, u32[]{:S(2)}) collective-permute-start(f32[1,3,8,2,12]{3,2,1,4,0:T(8,128)S(1)} %get-tuple-element.612), channel_id=1, source_target_pairs={{1,0},{2,1},{3,2},{5,4},{6,5},{7,6},{9,8},{10,9},{11,10},{13,12},{... | collective-permute-start | bytes 6920 | tf_op jit(solution)/shard_map/ppermute | solution.py:18
  293.5 86.0 %copy-start.4 = (bf16[144,6,128]{2,1,0:T(8,128)(2,1)S(1)}, bf16[144,6,128]{2,1,0:T(8,128)(2,1)}, u32[]{:S(2)}) copy-start(bf16[144,6,128]{2,1,0:T(8,128)(2,1)} %reshape.229) | copy-start | bytes 663556
  301.0 110.6 %all-to-all-start = ((f32[8,1,4608]{2,1,0:T(1,128)}), f32[8,1,4608]{2,1,0:T(1,128)}, u32[]{:S(2)}, u32[]{:S(2)}) async-start(f32[8,1,4608]{2,1,0:T(1,128)} %reshape.246), calls=%async_computation | async-start | bytes 294912 | tf_op jit(solution)/shard_map/all_to_all | solution.py:194
  408.1 2.3 copy-start.9
  429.5 2.2 copy-start.3
  433.6 2.0 copy-start.2
  444.8 2.2 copy-start.3
  460.2 2.2 copy-start.3
  475.6 2.2 copy-start.3
  490.9 2.2 copy-start.3
  506.3 2.2 copy-start.3
  521.7 2.2 copy-start.3
  537.0 2.2 copy-start.3
  (7 other events, 14.2 us)
Sparse Core Ops, SparseCore 0:
  10.0 84.7 all-gather.1
